TPU v7x, 256 devices: a whole 4x4x8 slice. The times are simulated.
256 devices in a mesh: dp: 2 (over core), ctx: 128 (over z, y, x).
Axes of the slice: x: 4, y: 4, z: 8, core: 2. Of those that a mesh axis runs over, the one named last changes fastest.
Arguments:
- hidden: bfloat16 [4, 16384, 5376], P('dp', 'ctx'), parts along dimension 0, may hold values from -400 to 400
- queries: bfloat16 [4, 16384, 2048], P('dp', 'ctx'), parts along dimension 0, may hold values from -400 to 400
- input_gain: float32 [5376], replicated, may hold values from 0.1 to 1.9
- kv_weight: bfloat16 [5376, 2048], P('ctx'), may hold values from -0.078125 to 0.078125
- query_gain: float32 [128], replicated, may hold values from 1 to 2.5
- key_gain: float32 [128], replicated, may hold values from 1 to 2.5
Outputs:
- attended: bfloat16 [4, 16384, 2048], P('dp', 'ctx'), parts along dimension 0
There are 2 independent parts, one for each index of `dp`. A program takes and returns all parts, laid end to end along the dimension named above; an argument that names none is the same for every part. Nothing has to cross between parts.
All inputs are finite; a program needn't handle non-finite values.
Results may differ from a plain program's by a relative error of at most 0.012.
Values may be sent and summed in bfloat16 or wider, within the bound.
A program may use at most 128 MiB of HBM per device.

v0:
```python
import jax
import jax.numpy as jnp
from jax import lax
from jax.sharding import PartitionSpec as P

HD = 128
WINDOW = 1024
attn_scalar = 168.0
norm_eps = 1e-06


def from_behind(block, axis, distance):
    devices = range(lax.axis_size(axis))
    route = [(i - distance, i) for i in devices if i - distance in devices]
    return lax.ppermute(block, axis, route)


def rotary_tables(positions, head_width):
    half_width = head_width // 2
    exponent = 2.0 * jnp.arange(half_width, dtype=jnp.float32) / head_width
    inverse = jnp.power(10000.0, -exponent)
    angles = positions.astype(jnp.float32)[:, None] * inverse[None, :]
    return (jnp.cos(angles), jnp.sin(angles))


def rotate(heads, cos_table, sine_table):
    half_width = heads.shape[-1] // 2
    first = heads[..., :half_width]
    second = heads[..., half_width:]
    cos_part = cos_table[:, None, :]
    sine_part = sine_table[:, None, :]
    return jnp.concatenate(
        [first * cos_part - second * sine_part, second * cos_part + first * sine_part], axis=-1
    )


def head_norm(heads, gain):
    return heads * lax.rsqrt(jnp.mean(heads * heads, axis=-1, keepdims=True) + norm_eps) * gain


def body(hidden, queries, input_gain, kv_weight, query_gain, key_gain):
    seq_count, block_len, model_width = hidden.shape
    kv_width = kv_weight.shape[1]
    kv_half = kv_width // 2
    kv_heads = kv_half // HD
    query_heads = queries.shape[2] // HD
    group_size = query_heads // kv_heads
    span_blocks = WINDOW // block_len
    token_rows = seq_count * block_len
    hidden_f32 = hidden.astype(jnp.float32)
    normed = (
        hidden_f32
        * lax.rsqrt(jnp.mean(hidden_f32 * hidden_f32, axis=-1, keepdims=True) + norm_eps)
        * input_gain
    )
    normed = normed.astype(jnp.bfloat16).reshape(token_rows, model_width)
    projected = jnp.dot(
        normed,
        lax.all_gather(kv_weight, "ctx", axis=0, tiled=True),
        preferred_element_type=jnp.float32,
    )
    key_proj = projected[:, :kv_half]
    value_proj = projected[:, kv_half:]
    shard_index = lax.axis_index("ctx")
    positions = shard_index * block_len + jnp.arange(block_len, dtype=jnp.int32)
    cos_table, sine_table = rotary_tables(positions, HD)
    key_part = key_proj.reshape(seq_count, block_len, kv_heads, HD)
    key_part = rotate(head_norm(key_part, key_gain), cos_table, sine_table).astype(jnp.bfloat16)
    value_part = value_proj.reshape(seq_count, block_len, kv_half).astype(jnp.bfloat16)
    key_block = jnp.concatenate(
        [key_part.reshape(seq_count, block_len, kv_half), value_part], axis=2
    )
    query_part = queries.astype(jnp.float32).reshape(seq_count, block_len, query_heads, HD)
    query_part = (
        rotate(head_norm(query_part, query_gain), cos_table, sine_table) * attn_scalar ** (-0.5)
    ).astype(jnp.bfloat16)
    previous = from_behind(key_block, "ctx", 1)
    pieces = [previous]
    for offset in range(2, span_blocks + 1):
        pieces.append(from_behind(key_block, "ctx", offset))
    window_blocks = jnp.concatenate(pieces[::-1] + [key_block], axis=1)
    key_pos = (shard_index - span_blocks) * block_len + jnp.arange(
        (span_blocks + 1) * block_len, dtype=jnp.int32
    )
    allowed = (
        (key_pos[None, :] <= positions[:, None])
        & (key_pos[None, :] > positions[:, None] - WINDOW)
        & (key_pos[None, :] >= 0)
    )
    outputs = []
    for seq_index in range(seq_count):
        window_keys = window_blocks[seq_index, :, :kv_half].reshape(-1, kv_heads, HD)
        window_values = window_blocks[seq_index, :, kv_half:].reshape(-1, kv_heads, HD)
        query_block = query_part[seq_index].reshape(block_len, kv_heads, group_size, HD)
        scores = jnp.einsum(
            "qhgd,khd->hgqk", query_block, window_keys, preferred_element_type=jnp.float32
        )
        weights = jnp.where(allowed, jnp.exp(scores), 0.0)
        row_total = jnp.sum(weights, axis=-1)
        weighted = jnp.einsum(
            "hgqk,khd->qhgd",
            weights.astype(jnp.bfloat16),
            window_values,
            preferred_element_type=jnp.float32,
        )
        result = weighted / jnp.transpose(row_total, (2, 0, 1))[..., None]
        outputs.append(result.astype(jnp.bfloat16).reshape(block_len, query_heads * HD))
    return jnp.stack(outputs, axis=0)


def solution(mesh):
    return jax.shard_map(
        body,
        mesh=mesh,
        in_specs=(P("dp", "ctx", None), P("dp", "ctx", None), P(), P("ctx", None), P(), P()),
        out_specs=P("dp", "ctx", None),
        check_vma=False,
    )
```

profile of v0, /device:TPU:64, one launch (start us, length us, event | category | flops | bytes accessed | tf_op | source)
XLA Modules:
  0.0 528.8 jit_solution(4616291720321876393)
XLA Ops:
  7.3 1.5 copy.71
  9.7 2.6 fusion.4
  13.4 2.2 fusion.6
  15.7 174.9 %all-gather.3.cloned.1.call-done = bf16[128,42,2048]{2,1,0:T(8,128)(2,1)} async-done(((bf16[1,42,2048]{2,1,0:T(8,128)(2,1)}), bf16[128,42,2048]{2,1,0:T(8,128)(2,1)}) %all-gather.3.cloned.1.call-update) | async-done | bytes 22020112 | tf_op jit(solution)/shard_map/all_gather | solution.py:59
  190.5 27.7 %reshape.131 = bf16[5376,2048]{1,0:T(8,128)(2,1)} reshape(bf16[128,42,2048]{2,1,0:T(8,128)(2,1)} %all-gather.3.cloned.1.call-done) | data formatting | bytes 44040192
  218.2 11.1 %fusion.35 = f32[256,2048]{1,0:T(8,128)S(1)} fusion(bf16[256,5376]{1,0:T(8,128)(2,1)} %bitcast.101, bf16[5376,2048]{1,0:T(8,128)(2,1)} %reshape.131), kind=kOutput, calls=%fused_computation.65 | convolution fusion | flops 5637144576 | bytes 26869760 | tf_op jit(solution)/shard_map/dot_general | solution.py:57
  231.4 1.6 copy.46
  233.0 1.3 add_rsqrt_fusion.1
  234.3 1.5 copy.47
  235.8 1.3 fusion.25
  238.2 1.3 copy.49
  239.6 4.9 collective-permute-start
  244.5 2.8 collective-permute-start.1
  247.3 1.4 fusion.16
  248.6 6.4 %collective-permute-start.2 = (bf16[2,128,2048]{1,2,0:T(8,128)(2,1)S(1)}, bf16[2,128,2048]{1,2,0:T(8,128)(2,1)S(1)}, u32[]{:S(2)}, u32[]{:S(2)}) collective-permute-start(bf16[2,128,2048]{1,2,0:T(8,128)(2,1)S(1)} %pad_maximum_fusion), channel_id=1, source_target_pairs={{0,6},{1,7},{2,8},{3,9},{4,10},{5,11},{6,12},{7,13},{8,14},{9,15},... | collective-permute-start | bytes 3145736 | tf_op jit(solution)/shard_map/ppermute | solution.py:15
  255.7 3.4 collective-permute-start.3
  259.7 3.1 collective-permute-start.4
  263.3 72.2 %collective-permute-done = bf16[2,128,2048]{1,2,0:T(8,128)(2,1)S(1)} collective-permute-done((bf16[2,128,2048]{1,2,0:T(8,128)(2,1)S(1)}, bf16[2,128,2048]{1,2,0:T(8,128)(2,1)S(1)}, u32[]{:S(2)}, u32[]{:S(2)}) %collective-permute-start) | collective-permute-done | bytes 1048608 | tf_op jit(solution)/shard_map/ppermute | solution.py:15
  335.5 5.4 %collective-permute-start.5 = (bf16[2,128,2048]{1,2,0:T(8,128)(2,1)S(1)}, bf16[2,128,2048]{1,2,0:T(8,128)(2,1)S(1)}, u32[]{:S(2)}, u32[]{:S(2)}) collective-permute-start(bf16[2,128,2048]{1,2,0:T(8,128)(2,1)S(1)} %pad_maximum_fusion), channel_id=1, source_target_pairs={{0,3},{1,4},{2,5},{3,6},{4,7},{5,8},{6,9},{7,10},{8,11},{9,12},{10... | collective-permute-start | bytes 3145736 | tf_op jit(solution)/shard_map/ppermute | solution.py:15
  341.1 23.2 %collective-permute-start.6 = (bf16[2,128,2048]{1,2,0:T(8,128)(2,1)S(1)}, bf16[2,128,2048]{1,2,0:T(8,128)(2,1)S(1)}, u32[]{:S(2)}, u32[]{:S(2)}) collective-permute-start(bf16[2,128,2048]{1,2,0:T(8,128)(2,1)S(1)} %pad_maximum_fusion), channel_id=1, source_target_pairs={{0,2},{1,3},{2,4},{3,5},{4,6},{5,7},{6,8},{7,9},{8,10},{9,11},{10,... | collective-permute-start | bytes 3145736 | tf_op jit(solution)/shard_map/ppermute | solution.py:15
  364.6 34.9 %collective-permute-start.7 = (bf16[2,128,2048]{1,2,0:T(8,128)(2,1)S(1)}, bf16[2,128,2048]{1,2,0:T(8,128)(2,1)S(1)}, u32[]{:S(2)}, u32[]{:S(2)}) collective-permute-start(bf16[2,128,2048]{1,2,0:T(8,128)(2,1)S(1)} %pad_maximum_fusion), channel_id=1, source_target_pairs={{0,1},{1,2},{2,3},{3,4},{4,5},{5,6},{6,7},{7,8},{8,9},{9,10},{10,1... | collective-permute-start | bytes 3145736 | tf_op jit(solution)/shard_map/ppermute | solution.py:15
  399.7 32.0 %collective-permute-done.3 = bf16[2,128,2048]{1,2,0:T(8,128)(2,1)S(1)} collective-permute-done((bf16[2,128,2048]{1,2,0:T(8,128)(2,1)S(1)}, bf16[2,128,2048]{1,2,0:T(8,128)(2,1)S(1)}, u32[]{:S(2)}, u32[]{:S(2)}) %collective-permute-start.3) | collective-permute-done | bytes 1048608 | tf_op jit(solution)/shard_map/ppermute | solution.py:15
  432.0 8.6 %collective-permute-done.4 = bf16[2,128,2048]{1,2,0:T(8,128)(2,1)S(1)} collective-permute-done((bf16[2,128,2048]{1,2,0:T(8,128)(2,1)S(1)}, bf16[2,128,2048]{1,2,0:T(8,128)(2,1)S(1)}, u32[]{:S(2)}, u32[]{:S(2)}) %collective-permute-start.4) | collective-permute-done | bytes 1048608 | tf_op jit(solution)/shard_map/ppermute | solution.py:15
  440.9 13.0 %collective-permute-done.5 = bf16[2,128,2048]{1,2,0:T(8,128)(2,1)S(1)} collective-permute-done((bf16[2,128,2048]{1,2,0:T(8,128)(2,1)S(1)}, bf16[2,128,2048]{1,2,0:T(8,128)(2,1)S(1)}, u32[]{:S(2)}, u32[]{:S(2)}) %collective-permute-start.5) | collective-permute-done | bytes 1048608 | tf_op jit(solution)/shard_map/ppermute | solution.py:15
  454.1 44.2 %collective-permute-done.6 = bf16[2,128,2048]{1,2,0:T(8,128)(2,1)S(1)} collective-permute-done((bf16[2,128,2048]{1,2,0:T(8,128)(2,1)S(1)}, bf16[2,128,2048]{1,2,0:T(8,128)(2,1)S(1)}, u32[]{:S(2)}, u32[]{:S(2)}) %collective-permute-start.6) | collective-permute-done | bytes 1048608 | tf_op jit(solution)/shard_map/ppermute | solution.py:15
  498.5 1.8 collective-permute-done.7
  500.8 2.0 fusion.33
  502.9 1.4 fusion.36
  504.3 3.6 fusion
  508.0 4.2 divide_convert_fusion.1
  513.4 6.2 %divide_convert_fusion = bf16[128,8,2,128]{0,3,2,1:T(8,128)(2,1)} fusion(bf16[1152,8,128,1]{0,2,3,1:T(8,128)(2,1)S(1)} %bitcast.102, f32[8,1152,128,2]{2,1,3,0:T(8,128)} %copy-done, pred[128,1152]{0,1:T(8,128)(4,1)S(1)} %and_and_fusion, f32[128,8,2]{0,2,1:T(2,128)S(1)} %bitcast.111), kind=kOutput, calls=%fused_computation.35 | convolution fusion | flops 609222656 | bytes 12476416 | tf_op jit(solution)/shard_map/hgqk,khd->qhgd/dot_general | solution.py:100
  519.7 1.2 copy.59
  (46 shorter events, 12.2 us)
Async XLA Ops:
  6.5 184.0 %all-gather.3.cloned.1.call-start = ((), (), s32[]{:S(2)}) async-start(), calls=%async_computation | async-start | bytes 25362432 | tf_op jit(solution)/shard_map/all_gather | solution.py:59
  8.7 4.7 copy-start.2
  9.6 3.9 copy-start.1
  239.6 96.0 %collective-permute-start = (bf16[2,128,2048]{1,2,0:T(8,128)(2,1)S(1)}, bf16[2,128,2048]{1,2,0:T(8,128)(2,1)S(1)}, u32[]{:S(2)}, u32[]{:S(2)}) collective-permute-start(bf16[2,128,2048]{1,2,0:T(8,128)(2,1)S(1)} %pad_maximum_fusion), channel_id=1, source_target_pairs={{0,8},{1,9},{2,10},{3,11},{4,12},{5,13},{6,14},{7,15},{8,16},{9,17... | collective-permute-start | bytes 3145736 | tf_op jit(solution)/shard_map/ppermute | solution.py:15
  244.5 96.6 %collective-permute-start.1 = (bf16[2,128,2048]{1,2,0:T(8,128)(2,1)S(1)}, bf16[2,128,2048]{1,2,0:T(8,128)(2,1)S(1)}, u32[]{:S(2)}, u32[]{:S(2)}) collective-permute-start(bf16[2,128,2048]{1,2,0:T(8,128)(2,1)S(1)} %pad_maximum_fusion), channel_id=1, source_target_pairs={{0,7},{1,8},{2,9},{3,10},{4,11},{5,12},{6,13},{7,14},{8,15},{9,16}... | collective-permute-start | bytes 3145736 | tf_op jit(solution)/shard_map/ppermute | solution.py:15
  248.6 115.9 %collective-permute-start.2 = (bf16[2,128,2048]{1,2,0:T(8,128)(2,1)S(1)}, bf16[2,128,2048]{1,2,0:T(8,128)(2,1)S(1)}, u32[]{:S(2)}, u32[]{:S(2)}) collective-permute-start(bf16[2,128,2048]{1,2,0:T(8,128)(2,1)S(1)} %pad_maximum_fusion), channel_id=1, source_target_pairs={{0,6},{1,7},{2,8},{3,9},{4,10},{5,11},{6,12},{7,13},{8,14},{9,15},... | collective-permute-start | bytes 3145736 | tf_op jit(solution)/shard_map/ppermute | solution.py:15
  255.7 176.1 %collective-permute-start.3 = (bf16[2,128,2048]{1,2,0:T(8,128)(2,1)S(1)}, bf16[2,128,2048]{1,2,0:T(8,128)(2,1)S(1)}, u32[]{:S(2)}, u32[]{:S(2)}) collective-permute-start(bf16[2,128,2048]{1,2,0:T(8,128)(2,1)S(1)} %pad_maximum_fusion), channel_id=1, source_target_pairs={{0,5},{1,6},{2,7},{3,8},{4,9},{5,10},{6,11},{7,12},{8,13},{9,14},{... | collective-permute-start | bytes 3145736 | tf_op jit(solution)/shard_map/ppermute | solution.py:15
  259.7 180.9 %collective-permute-start.4 = (bf16[2,128,2048]{1,2,0:T(8,128)(2,1)S(1)}, bf16[2,128,2048]{1,2,0:T(8,128)(2,1)S(1)}, u32[]{:S(2)}, u32[]{:S(2)}) collective-permute-start(bf16[2,128,2048]{1,2,0:T(8,128)(2,1)S(1)} %pad_maximum_fusion), channel_id=1, source_target_pairs={{0,4},{1,5},{2,6},{3,7},{4,8},{5,9},{6,10},{7,11},{8,12},{9,13},{1... | collective-permute-start | bytes 3145736 | tf_op jit(solution)/shard_map/ppermute | solution.py:15
  335.5 118.3 %collective-permute-start.5 = (bf16[2,128,2048]{1,2,0:T(8,128)(2,1)S(1)}, bf16[2,128,2048]{1,2,0:T(8,128)(2,1)S(1)}, u32[]{:S(2)}, u32[]{:S(2)}) collective-permute-start(bf16[2,128,2048]{1,2,0:T(8,128)(2,1)S(1)} %pad_maximum_fusion), channel_id=1, source_target_pairs={{0,3},{1,4},{2,5},{3,6},{4,7},{5,8},{6,9},{7,10},{8,11},{9,12},{10... | collective-permute-start | bytes 3145736 | tf_op jit(solution)/shard_map/ppermute | solution.py:15
  341.1 157.2 %collective-permute-start.6 = (bf16[2,128,2048]{1,2,0:T(8,128)(2,1)S(1)}, bf16[2,128,2048]{1,2,0:T(8,128)(2,1)S(1)}, u32[]{:S(2)}, u32[]{:S(2)}) collective-permute-start(bf16[2,128,2048]{1,2,0:T(8,128)(2,1)S(1)} %pad_maximum_fusion), channel_id=1, source_target_pairs={{0,2},{1,3},{2,4},{3,5},{4,6},{5,7},{6,8},{7,9},{8,10},{9,11},{10,... | collective-permute-start | bytes 3145736 | tf_op jit(solution)/shard_map/ppermute | solution.py:15
  364.6 135.7 %collective-permute-start.7 = (bf16[2,128,2048]{1,2,0:T(8,128)(2,1)S(1)}, bf16[2,128,2048]{1,2,0:T(8,128)(2,1)S(1)}, u32[]{:S(2)}, u32[]{:S(2)}) collective-permute-start(bf16[2,128,2048]{1,2,0:T(8,128)(2,1)S(1)} %pad_maximum_fusion), channel_id=1, source_target_pairs={{0,1},{1,2},{2,3},{3,4},{4,5},{5,6},{6,7},{7,8},{8,9},{9,10},{10,1... | collective-permute-start | bytes 3145736 | tf_op jit(solution)/shard_map/ppermute | solution.py:15
  504.3 3.7 copy-start
Sparse Core Ops, SparseCore 0:
  11.0 179.4 all-gather.2
where the time goes:
time: 530 us; the launch traced here: 529 us
  waiting for transfers between devices  347 us (65%)
  starting transfers between devices  84 us (16%)
  local copies, waits for them, and re-layouts  42.1 us (8%)
  matrix products  26.6 us (5%)
  other arithmetic  14.9 us (3%)
  between operations  13.8 us (3%)
    all_gather x1, waiting for transfers between devices, body(): lax.all_gather(kv_weight, 'ctx', axis=0, tiled=True)  175 us
    ppermute x8, waiting for transfers between devices, from_behind(): return lax.ppermute(block, axis, route)  172 us
    ppermute x8, starting transfers between devices, from_behind(): return lax.ppermute(block, axis, route)  84 us
    unnamed x18, local copies, waits for them, and re-layouts  31.4 us
    dot_general x1, matrix products, body(): jnp.dot(normed, lax.all_gather(kv_weight, 'ctx', axis=0, tiled=True), pre...  11.1 us
  transfers between devices with their start and end apart: 9, of which 7 were waited for; matrix products, arithmetic and copies ran while one was open for 2% of the time, Pallas kernels for 0%

commit v1 on v0

--- a/solution.py
+++ b/solution.py
@@ -56,7 +56,9 @@
     normed = normed.astype(jnp.bfloat16).reshape(token_rows, model_width)
     projected = jnp.dot(
         normed,
-        lax.all_gather(kv_weight, "ctx", axis=0, tiled=True),
+        jnp.concatenate(
+            lax.all_to_all(jnp.stack([kv_weight] * lax.axis_size("ctx")), "ctx", 0, 0), axis=0
+        ),
         preferred_element_type=jnp.float32,
     )
     key_proj = projected[:, :kv_half]

time: 530 us -> 931 us (1.76)
  the two profiles are of different devices: /device:TPU:64 before, /device:TPU:160 now
where the time goes in v1:
time: 931 us; the launch traced here: 930 us
  waiting for transfers between devices  748 us (80%)
  starting transfers between devices  89 us (10%)
  local copies, waits for them, and re-layouts  50.3 us (5%)
  matrix products  26.6 us (3%)
  other arithmetic  14.9 us (2%)
    all_to_all x1, waiting for transfers between devices, body(): lax.all_to_all(jnp.stack([kv_weight] * lax.axis_size('ctx')), 'ctx', 0, 0)  557 us
    ppermute x8, waiting for transfers between devices, from_behind(): return lax.ppermute(block, axis, route)  191 us
    ppermute x8, starting transfers between devices, from_behind(): return lax.ppermute(block, axis, route)  74.8 us
    reshape x1, local copies, waits for them, and re-layouts, body(): jnp.concatenate(lax.all_to_all(jnp.stack([kv_weight] * lax.axis_size('ctx...  27.7 us
  transfers between devices with their start and end apart: 9, of which 7 were waited for; matrix products, arithmetic and copies ran while one was open for 1% of the time, Pallas kernels for 0%

profile of v1, /device:TPU:160, one launch (start us, length us, event | category | flops | bytes accessed | tf_op | source)
XLA Modules:
  0.0 929.5 jit_solution(9349696965694032198)
XLA Ops:
  0.0 9.3 %stack.4 = bf16[128,42,2048]{2,1,0:T(8,128)(2,1)} broadcast(bf16[42,2048]{1,0:T(8,128)(2,1)} %param.9), dimensions={1,2} | broadcast | bytes 22192128 | tf_op jit(solution)/shard_map/stack | solution.py:60
  9.3 14.1 %all-to-all-start = ((bf16[128,42,2048]{2,1,0:T(8,128)(2,1)}), bf16[128,42,2048]{2,1,0:T(8,128)(2,1)}, u32[]{:S(2)}, u32[]{:S(2)}) async-start(bf16[128,42,2048]{2,1,0:T(8,128)(2,1)} %stack.4), calls=%async_computation | async-start | bytes 50331648 | tf_op jit(solution)/shard_map/all_to_all | solution.py:60
  24.7 2.6 fusion.4
  28.5 2.2 fusion.6
  30.7 557.4 %all-to-all-done = bf16[128,42,2048]{2,1,0:T(8,128)(2,1)} async-done(((bf16[128,42,2048]{2,1,0:T(8,128)(2,1)}), bf16[128,42,2048]{2,1,0:T(8,128)(2,1)}, u32[]{:S(2)}, u32[]{:S(2)}) %all-to-all-start) | async-done | bytes 22020128 | tf_op jit(solution)/shard_map/all_to_all | solution.py:60
  588.1 27.7 %reshape.130 = bf16[5376,2048]{1,0:T(8,128)(2,1)} reshape(bf16[128,42,2048]{2,1,0:T(8,128)(2,1)} %all-to-all-done) | data formatting | bytes 44040192 | tf_op jit(solution)/shard_map/reshape | solution.py:59
  615.8 11.1 %fusion.35 = f32[256,2048]{1,0:T(8,128)S(1)} fusion(bf16[256,5376]{1,0:T(8,128)(2,1)} %bitcast.100, bf16[5376,2048]{1,0:T(8,128)(2,1)} %reshape.130), kind=kOutput, calls=%fused_computation.65 | convolution fusion | flops 5637144576 | bytes 26869760 | tf_op jit(solution)/shard_map/dot_general | solution.py:57
  629.0 1.6 copy.46
  630.6 1.3 add_rsqrt_fusion.1
  631.8 1.5 copy.47
  633.3 1.3 fusion.25
  635.7 1.3 copy.49
  637.1 9.0 collective-permute-start
  646.1 1.9 collective-permute-start.1
  648.0 1.4 fusion.16
  649.4 1.9 collective-permute-start.2
  652.0 3.4 collective-permute-start.3
  656.0 11.1 %collective-permute-start.4 = (bf16[2,128,2048]{1,2,0:T(8,128)(2,1)S(1)}, bf16[2,128,2048]{1,2,0:T(8,128)(2,1)S(1)}, u32[]{:S(2)}, u32[]{:S(2)}) collective-permute-start(bf16[2,128,2048]{1,2,0:T(8,128)(2,1)S(1)} %pad_maximum_fusion), channel_id=1, source_target_pairs={{0,4},{1,5},{2,6},{3,7},{4,8},{5,9},{6,10},{7,11},{8,12},{9,13},{1... | collective-permute-start | bytes 3145736 | tf_op jit(solution)/shard_map/ppermute | solution.py:15
  667.7 69.5 %collective-permute-done = bf16[2,128,2048]{1,2,0:T(8,128)(2,1)S(1)} collective-permute-done((bf16[2,128,2048]{1,2,0:T(8,128)(2,1)S(1)}, bf16[2,128,2048]{1,2,0:T(8,128)(2,1)S(1)}, u32[]{:S(2)}, u32[]{:S(2)}) %collective-permute-start) | collective-permute-done | bytes 1048608 | tf_op jit(solution)/shard_map/ppermute | solution.py:15
  737.2 2.9 collective-permute-start.5
  740.2 20.3 %collective-permute-start.6 = (bf16[2,128,2048]{1,2,0:T(8,128)(2,1)S(1)}, bf16[2,128,2048]{1,2,0:T(8,128)(2,1)S(1)}, u32[]{:S(2)}, u32[]{:S(2)}) collective-permute-start(bf16[2,128,2048]{1,2,0:T(8,128)(2,1)S(1)} %pad_maximum_fusion), channel_id=1, source_target_pairs={{0,2},{1,3},{2,4},{3,5},{4,6},{5,7},{6,8},{7,9},{8,10},{9,11},{10,... | collective-permute-start | bytes 3145736 | tf_op jit(solution)/shard_map/ppermute | solution.py:15
  760.8 24.3 %collective-permute-start.7 = (bf16[2,128,2048]{1,2,0:T(8,128)(2,1)S(1)}, bf16[2,128,2048]{1,2,0:T(8,128)(2,1)S(1)}, u32[]{:S(2)}, u32[]{:S(2)}) collective-permute-start(bf16[2,128,2048]{1,2,0:T(8,128)(2,1)S(1)} %pad_maximum_fusion), channel_id=1, source_target_pairs={{0,1},{1,2},{2,3},{3,4},{4,5},{5,6},{6,7},{7,8},{8,9},{9,10},{10,1... | collective-permute-start | bytes 3145736 | tf_op jit(solution)/shard_map/ppermute | solution.py:15
  785.3 36.8 %collective-permute-done.3 = bf16[2,128,2048]{1,2,0:T(8,128)(2,1)S(1)} collective-permute-done((bf16[2,128,2048]{1,2,0:T(8,128)(2,1)S(1)}, bf16[2,128,2048]{1,2,0:T(8,128)(2,1)S(1)}, u32[]{:S(2)}, u32[]{:S(2)}) %collective-permute-start.3) | collective-permute-done | bytes 1048608 | tf_op jit(solution)/shard_map/ppermute | solution.py:15
  822.4 28.2 %collective-permute-done.4 = bf16[2,128,2048]{1,2,0:T(8,128)(2,1)S(1)} collective-permute-done((bf16[2,128,2048]{1,2,0:T(8,128)(2,1)S(1)}, bf16[2,128,2048]{1,2,0:T(8,128)(2,1)S(1)}, u32[]{:S(2)}, u32[]{:S(2)}) %collective-permute-start.4) | collective-permute-done | bytes 1048608 | tf_op jit(solution)/shard_map/ppermute | solution.py:15
  850.9 5.7 collective-permute-done.5
  856.8 45.3 %collective-permute-done.6 = bf16[2,128,2048]{1,2,0:T(8,128)(2,1)S(1)} collective-permute-done((bf16[2,128,2048]{1,2,0:T(8,128)(2,1)S(1)}, bf16[2,128,2048]{1,2,0:T(8,128)(2,1)S(1)}, u32[]{:S(2)}, u32[]{:S(2)}) %collective-permute-start.6) | collective-permute-done | bytes 1048608 | tf_op jit(solution)/shard_map/ppermute | solution.py:15
  902.4 5.5 collective-permute-done.7
  908.4 2.0 fusion.33
  910.4 1.4 fusion.36
  911.9 3.6 fusion
  915.5 4.2 divide_convert_fusion.1
  921.0 6.2 divide_convert_fusion
  (48 shorter events, 13.0 us)
Async XLA Ops:
  9.3 14.2 %copy-start.2 = (bf16[2,128,2048]{2,1,0:T(8,128)(2,1)S(1)}, bf16[2,128,2048]{2,1,0:T(8,128)(2,1)}, u32[]{:S(2)}) copy-start(bf16[2,128,2048]{2,1,0:T(8,128)(2,1)} %param.7) | copy-start | bytes 3145732
  9.3 578.7 %all-to-all-start = ((bf16[128,42,2048]{2,1,0:T(8,128)(2,1)}), bf16[128,42,2048]{2,1,0:T(8,128)(2,1)}, u32[]{:S(2)}, u32[]{:S(2)}) async-start(bf16[128,42,2048]{2,1,0:T(8,128)(2,1)} %stack.4), calls=%async_computation | async-start | bytes 50331648 | tf_op jit(solution)/shard_map/all_to_all | solution.py:60
  23.8 4.7 copy-start.3
  24.6 3.9 copy-start.1
  637.1 100.0 %collective-permute-start = (bf16[2,128,2048]{1,2,0:T(8,128)(2,1)S(1)}, bf16[2,128,2048]{1,2,0:T(8,128)(2,1)S(1)}, u32[]{:S(2)}, u32[]{:S(2)}) collective-permute-start(bf16[2,128,2048]{1,2,0:T(8,128)(2,1)S(1)} %pad_maximum_fusion), channel_id=1, source_target_pairs={{0,8},{1,9},{2,10},{3,11},{4,12},{5,13},{6,14},{7,15},{8,16},{9,17... | collective-permute-start | bytes 3145736 | tf_op jit(solution)/shard_map/ppermute | solution.py:15
  646.1 94.1 %collective-permute-start.1 = (bf16[2,128,2048]{1,2,0:T(8,128)(2,1)S(1)}, bf16[2,128,2048]{1,2,0:T(8,128)(2,1)S(1)}, u32[]{:S(2)}, u32[]{:S(2)}) collective-permute-start(bf16[2,128,2048]{1,2,0:T(8,128)(2,1)S(1)} %pad_maximum_fusion), channel_id=1, source_target_pairs={{0,7},{1,8},{2,9},{3,10},{4,11},{5,12},{6,13},{7,14},{8,15},{9,16}... | collective-permute-start | bytes 3145736 | tf_op jit(solution)/shard_map/ppermute | solution.py:15
  649.4 111.4 %collective-permute-start.2 = (bf16[2,128,2048]{1,2,0:T(8,128)(2,1)S(1)}, bf16[2,128,2048]{1,2,0:T(8,128)(2,1)S(1)}, u32[]{:S(2)}, u32[]{:S(2)}) collective-permute-start(bf16[2,128,2048]{1,2,0:T(8,128)(2,1)S(1)} %pad_maximum_fusion), channel_id=1, source_target_pairs={{0,6},{1,7},{2,8},{3,9},{4,10},{5,11},{6,12},{7,13},{8,14},{9,15},... | collective-permute-start | bytes 3145736 | tf_op jit(solution)/shard_map/ppermute | solution.py:15
  652.0 170.2 %collective-permute-start.3 = (bf16[2,128,2048]{1,2,0:T(8,128)(2,1)S(1)}, bf16[2,128,2048]{1,2,0:T(8,128)(2,1)S(1)}, u32[]{:S(2)}, u32[]{:S(2)}) collective-permute-start(bf16[2,128,2048]{1,2,0:T(8,128)(2,1)S(1)} %pad_maximum_fusion), channel_id=1, source_target_pairs={{0,5},{1,6},{2,7},{3,8},{4,9},{5,10},{6,11},{7,12},{8,13},{9,14},{... | collective-permute-start | bytes 3145736 | tf_op jit(solution)/shard_map/ppermute | solution.py:15
  656.0 194.6 %collective-permute-start.4 = (bf16[2,128,2048]{1,2,0:T(8,128)(2,1)S(1)}, bf16[2,128,2048]{1,2,0:T(8,128)(2,1)S(1)}, u32[]{:S(2)}, u32[]{:S(2)}) collective-permute-start(bf16[2,128,2048]{1,2,0:T(8,128)(2,1)S(1)} %pad_maximum_fusion), channel_id=1, source_target_pairs={{0,4},{1,5},{2,6},{3,7},{4,8},{5,9},{6,10},{7,11},{8,12},{9,13},{1... | collective-permute-start | bytes 3145736 | tf_op jit(solution)/shard_map/ppermute | solution.py:15
  737.2 119.4 %collective-permute-start.5 = (bf16[2,128,2048]{1,2,0:T(8,128)(2,1)S(1)}, bf16[2,128,2048]{1,2,0:T(8,128)(2,1)S(1)}, u32[]{:S(2)}, u32[]{:S(2)}) collective-permute-start(bf16[2,128,2048]{1,2,0:T(8,128)(2,1)S(1)} %pad_maximum_fusion), channel_id=1, source_target_pairs={{0,3},{1,4},{2,5},{3,6},{4,7},{5,8},{6,9},{7,10},{8,11},{9,12},{10... | collective-permute-start | bytes 3145736 | tf_op jit(solution)/shard_map/ppermute | solution.py:15
  740.2 161.9 %collective-permute-start.6 = (bf16[2,128,2048]{1,2,0:T(8,128)(2,1)S(1)}, bf16[2,128,2048]{1,2,0:T(8,128)(2,1)S(1)}, u32[]{:S(2)}, u32[]{:S(2)}) collective-permute-start(bf16[2,128,2048]{1,2,0:T(8,128)(2,1)S(1)} %pad_maximum_fusion), channel_id=1, source_target_pairs={{0,2},{1,3},{2,4},{3,5},{4,6},{5,7},{6,8},{7,9},{8,10},{9,11},{10,... | collective-permute-start | bytes 3145736 | tf_op jit(solution)/shard_map/ppermute | solution.py:15
  760.8 147.1 %collective-permute-start.7 = (bf16[2,128,2048]{1,2,0:T(8,128)(2,1)S(1)}, bf16[2,128,2048]{1,2,0:T(8,128)(2,1)S(1)}, u32[]{:S(2)}, u32[]{:S(2)}) collective-permute-start(bf16[2,128,2048]{1,2,0:T(8,128)(2,1)S(1)} %pad_maximum_fusion), channel_id=1, source_target_pairs={{0,1},{1,2},{2,3},{3,4},{4,5},{5,6},{6,7},{7,8},{8,9},{9,10},{10,1... | collective-permute-start | bytes 3145736 | tf_op jit(solution)/shard_map/ppermute | solution.py:15
  911.8 3.7 copy-start
